TPU v7x, 256 devices: a whole 4x4x8 slice. The times are simulated.
256 devices in a mesh: dp: 16 (over y, x), vocab: 16 (over z, core).
Axes of the slice: x: 4, y: 4, z: 8, core: 2. Of those that a mesh axis runs over, the one named last changes fastest.
Arguments:
- hidden: bfloat16 [256, 128, 4096], P('vocab', None, 'dp'), may hold values from -6 to 6
- weights: bfloat16 [65536, 4096], P('vocab', 'dp'), may hold values from -0.09375 to 0.09375
- bias: float32 [65536], P('vocab'), may hold values from -4 to 4
- first_moment: bfloat16 [65536, 4096], P('vocab', 'dp'), may hold values from -6 to 6
- second_moment: bfloat16 [65536, 4096], P('vocab', 'dp'), may hold values from 0.049804688 to 2
- rep_cot: bfloat16 [256, 16, 512], P(None, 'vocab'), may hold values from -768 to 768
- active_blocks: int32 [256, 16, 4], P(None, 'vocab'), may hold values from 0 to 31, as said below
- block_counts: int32 [256, 16], replicated, may hold values from 0 to 4, as said below
- passage_len: int32 [256], replicated, may hold values from 16 to 128, as said below
Outputs:
- reps: float32 [16, 16, 4, 512], P('dp', 'vocab')
- grad_hidden: bfloat16 [256, 128, 4096], P('vocab', None, 'dp')
- new_first: bfloat16 [65536, 4096], P('vocab', 'dp')
- new_second: bfloat16 [65536, 4096], P('vocab', 'dp')
Inputs may be any that keep to these rules, and one draw needn't show every extreme that they name: `block_counts`: within each batch of 16 passages, every owner has between max(1, 2) and 4 live passages, and in every batch some owner has exactly 4; some passage at each owner of each batch has count 4. `active_blocks`: the 4 block numbers of one passage at one owner are distinct. `passage_len`: every batch has a passage of length 128.
All inputs are finite; a program needn't handle non-finite values.
Results may differ from a plain program's by a relative error of at most 0.012.
Values may be sent and summed in bfloat16 or wider, within the bound.
No kernel may reach another device: no remote copies, remote signals or barrier semaphores. Data moves between devices by JAX's collectives and lax.ppermute only.
A program may use at most 128 MiB of HBM per device.

v0:
```python
import jax
import jax.numpy as jnp
from jax import lax
from jax.sharding import PartitionSpec as P

BLOCK = 128
OWN_BLOCKS = 32
SLOT_BLOCKS = 4
OWN_SLOTS = 4
beta_one = 0.9
beta_two = 0.999


def slot_tables(block_counts, batches, owners, per_batch, slot_total):
    live_mask = (block_counts > 0).astype(jnp.int32).reshape(batches, per_batch, owners)
    slot_rank = jnp.cumsum(live_mask, axis=1, dtype=jnp.int32) - live_mask
    slot_place = jnp.arange(slot_total, dtype=jnp.int32)
    chosen = (live_mask[:, :, :, None] == 1) & (
        slot_rank[:, :, :, None] == slot_place[None, None, None, :]
    )
    return jnp.transpose(chosen, (0, 2, 3, 1)).astype(jnp.int32)


def slot_info(onehot, ids_col, counts_col, lengths, plen_size, block_size):
    slot_ids = jnp.sum(onehot[:, :, :, None] * ids_col[:, None, :, :], axis=2)
    slot_count = jnp.sum(onehot * counts_col[:, None, :], axis=2)
    slot_len = jnp.sum(onehot * lengths[:, None, :], axis=2)
    filled = jnp.sum(onehot, axis=2)
    divisor = jnp.where(filled > 0, slot_len, 1).astype(jnp.float32)
    token_ok = jnp.arange(plen_size, dtype=jnp.int32)[None, None, :] < slot_len[:, :, None]
    col_block = jnp.arange(slot_ids.shape[2] * block_size, dtype=jnp.int32) // block_size
    col_ok = col_block[None, None, :] < slot_count[:, :, None]
    return (slot_ids, divisor, token_ok, col_ok)


def activate(logits, bias_cols, cot, token_ok, col_ok, divisor):
    shifted = logits + bias_cols[:, :, None, :]
    softened = jax.nn.softplus(shifted)
    kept_mask = (token_ok[:, :, :, None] & col_ok[:, :, None, :]).astype(jnp.float32)
    pool_weight = kept_mask / divisor[:, :, None, None]
    pooled = jnp.sum(jnp.log1p(softened) * pool_weight, axis=2)
    slope = (cot[:, :, None, :] * pool_weight * jax.nn.sigmoid(shifted) / (1.0 + softened)).astype(
        jnp.bfloat16
    )
    return (pooled, slope)


def shards(
    hidden,
    weights,
    bias,
    first_moment,
    second_moment,
    rep_cot,
    active_blocks,
    block_counts,
    passage_len,
):
    owners = lax.axis_size("vocab")
    feature_parts = lax.axis_size("dp")
    per_batch, plen_size, dslice = hidden.shape
    col_width = SLOT_BLOCKS * BLOCK
    my_batch = lax.axis_index("vocab")
    chosen = slot_tables(block_counts, owners, owners, per_batch, OWN_SLOTS)
    my_slots = lax.dynamic_index_in_dim(chosen, my_batch, 0, keepdims=False)
    pick_rows = my_slots.reshape(owners * OWN_SLOTS, per_batch).astype(jnp.bfloat16)
    outgoing = jnp.dot(
        pick_rows, hidden.reshape(per_batch, plen_size * dslice), preferred_element_type=jnp.float32
    )
    outgoing = outgoing.astype(jnp.bfloat16).reshape(owners, OWN_SLOTS, plen_size, dslice)
    arrived = lax.all_to_all(outgoing, "vocab", split_axis=0, concat_axis=0, tiled=True)
    onehot = lax.dynamic_index_in_dim(chosen, my_batch, 1, keepdims=False)
    ids_col = active_blocks.reshape(owners, per_batch, SLOT_BLOCKS)
    counts_col = lax.dynamic_index_in_dim(block_counts, my_batch, 1, keepdims=False).reshape(
        owners, per_batch
    )
    lengths = passage_len.reshape(owners, per_batch)
    slot_ids, divisor, token_ok, col_ok = slot_info(
        onehot, ids_col, counts_col, lengths, plen_size, BLOCK
    )
    cot_col = rep_cot.reshape(owners, per_batch, col_width).astype(jnp.float32)
    slot_cot = jnp.einsum("jsp,jpc->jsc", onehot.astype(jnp.float32), cot_col)
    w_blocks = weights.reshape(OWN_BLOCKS, BLOCK, dslice)
    bias_blocks = bias.reshape(OWN_BLOCKS, BLOCK)
    bias_cols = bias_blocks[slot_ids].reshape(owners, OWN_SLOTS, col_width)

    def partial_for(inputs_here):
        slot_rows, block_ids = inputs_here
        w_sel = w_blocks[block_ids].reshape(OWN_SLOTS, col_width, dslice)
        return jnp.einsum(
            "std,scd->stc", slot_rows, w_sel, preferred_element_type=jnp.float32
        ).astype(jnp.bfloat16)

    partial_value = lax.map(partial_for, (arrived, slot_ids))
    my_share = owners // feature_parts
    my_start = lax.axis_index("dp") * my_share
    logits_mine = lax.psum_scatter(partial_value, "dp", scatter_dimension=0, tiled=True).astype(
        jnp.float32
    )
    pooled_mine, slope_mine = activate(
        logits_mine,
        lax.dynamic_slice_in_dim(bias_cols, my_start, my_share, 0),
        lax.dynamic_slice_in_dim(slot_cot, my_start, my_share, 0),
        lax.dynamic_slice_in_dim(token_ok, my_start, my_share, 0),
        lax.dynamic_slice_in_dim(col_ok, my_start, my_share, 0),
        lax.dynamic_slice_in_dim(divisor, my_start, my_share, 0),
    )
    slope_all = lax.all_gather(slope_mine, "dp", axis=0, tiled=True)

    def backward_step(grad_sum, inputs_here):
        slot_rows, block_ids, slope = inputs_here
        w_sel = w_blocks[block_ids].reshape(OWN_SLOTS, col_width, dslice)
        back_part = jnp.einsum(
            "stc,scd->std", slope, w_sel, preferred_element_type=jnp.float32
        ).astype(jnp.bfloat16)
        outer_sum = jnp.einsum("std,stc->scd", slot_rows, slope, preferred_element_type=jnp.float32)
        grad_sum = grad_sum.at[block_ids.reshape(-1)].add(
            outer_sum.reshape(OWN_SLOTS * SLOT_BLOCKS, BLOCK, dslice)
        )
        return (grad_sum, back_part)

    start_grad = jnp.zeros((OWN_BLOCKS, BLOCK, dslice), jnp.float32)
    grad_blocks, returned = lax.scan(backward_step, start_grad, (arrived, slot_ids, slope_all))
    back_home = lax.all_to_all(returned, "vocab", split_axis=0, concat_axis=0, tiled=True)
    gathered = jnp.dot(
        pick_rows.T,
        back_home.reshape(owners * OWN_SLOTS, plen_size * dslice),
        preferred_element_type=jnp.float32,
    )
    grad_hidden = gathered.reshape(per_batch, plen_size, dslice).astype(jnp.bfloat16)
    grad_w = grad_blocks.reshape(OWN_BLOCKS * BLOCK, dslice)
    new_first = (beta_one * first_moment.astype(jnp.float32) + (1.0 - beta_one) * grad_w).astype(
        jnp.bfloat16
    )
    new_second = (
        beta_two * second_moment.astype(jnp.float32) + (1.0 - beta_two) * grad_w * grad_w
    ).astype(jnp.bfloat16)
    reps = pooled_mine[:, None, :, :]
    return (reps, grad_hidden, new_first, new_second)


def solution(mesh):
    return jax.shard_map(
        shards,
        mesh=mesh,
        in_specs=(
            P("vocab", None, "dp"),
            P("vocab", "dp"),
            P("vocab"),
            P("vocab", "dp"),
            P("vocab", "dp"),
            P(None, "vocab", None),
            P(None, "vocab", None),
            P(),
            P(),
        ),
        out_specs=(
            P("dp", "vocab", None, None),
            P("vocab", None, "dp"),
            P("vocab", "dp"),
            P("vocab", "dp"),
        ),
        check_vma=False,
    )
```

profile of v0, /device:TPU:1, one launch (start us, length us, event | category | flops | bytes accessed | tf_op | source)
XLA Modules:
  0.0 653.8 jit_solution(12631458405986258486)
XLA Ops:
  12.3 3.0 copy.65
  15.3 10.1 %all-to-all-start = ((bf16[16,4,128,256]{3,2,1,0:T(8,128)(2,1)}), bf16[16,4,128,256]{3,2,1,0:T(8,128)(2,1)}, u32[]{:S(2)}, u32[]{:S(2)}) async-start(bf16[16,4,128,256]{3,2,1,0:T(8,128)(2,1)} %bitcast.132), calls=%async_computation | async-start | bytes 8388608 | tf_op jit(solution)/shard_map/all_to_all | solution.py:71
  27.6 91.4 %all-to-all-done = bf16[16,4,128,256]{3,2,1,0:T(8,128)(2,1)} async-done(((bf16[16,4,128,256]{3,2,1,0:T(8,128)(2,1)}), bf16[16,4,128,256]{3,2,1,0:T(8,128)(2,1)}, u32[]{:S(2)}, u32[]{:S(2)}) %all-to-all-start) | async-done | bytes 4194336 | tf_op jit(solution)/shard_map/all_to_all | solution.py:71
  119.0 78.0 %while.22 = (s32[]{:T(128)}, bf16[16,4,128,512]{2,3,1,0:T(8,128)(2,1)}, bf16[16,4,128,256]{3,2,1,0:T(8,128)(2,1)}, s32[16,4,4]{2,1,0:T(4,128)S(1)}, bf16[32,128,256]{2,1,0:T(8,128)(2,1)}, /*index=5*/s32[]{:T(128)}) while((s32[]{:T(128)}, bf16[16,4,128,512]{2,3,1,0:T(8,128)(2,1)}, bf16[16,4,128,256]{3,2,1,0:T(8,128)(2,1)}, ...), condition=%wide.region_3.4_spmd, body=%wide.region_2.3_spmd.sunk | while | flops 134480944 | bytes 6033881 | solution.py:94
  119.1 2.2 gather_fusion
  143.4 2.2 gather_fusion
  148.3 2.2 gather_fusion
  199.2 86.7 %reduce-scatter.4.cloned.1.call-done = bf16[1,4,128,512]{2,3,1,0:T(8,128)(2,1)} async-done(((bf16[16,4,128,512]{2,3,1,0:T(8,128)(2,1)}), bf16[1,4,128,512]{2,3,1,0:T(8,128)(2,1)}) %reduce-scatter.4.cloned.1.call-update) | async-done | bytes 524304
  285.9 4.0 divide_convert_fusion
  291.0 76.7 %all-gather.2.cloned.1.call-done = bf16[16,4,128,512]{3,2,1,0:T(8,128)(2,1)} async-done(((bf16[1,4,128,512]{3,2,1,0:T(8,128)(2,1)}), bf16[16,4,128,512]{3,2,1,0:T(8,128)(2,1)}) %all-gather.2.cloned.1.call-update) | async-done | bytes 8388624 | tf_op jit(solution)/shard_map/all_gather | solution.py:108
  367.6 2.4 broadcast_in_dim.23
  370.1 168.9 %while.23 = (s32[]{:T(128)}, f32[32,128,256]{2,1,0:T(8,128)}, bf16[16,4,128,256]{3,2,1,0:T(8,128)(2,1)}, s32[16,4,4]{2,1,0:T(4,128)S(1)}, bf16[16,4,128,512]{3,2...) while((s32[]{:T(128)}, f32[32,128,256]{2,1,0:T(8,128)}, ...), condition=%wide.region_11.12_spmd, body=%wide.region_9.11_spmd.sunk | while | flops 269091936 | bytes 13114209 | solution.py:123
  371.8 4.5 scatter_fusion
  382.3 4.4 scatter_fusion
  392.8 4.6 scatter_fusion
  403.5 4.6 scatter_fusion
  414.2 4.4 scatter_fusion
  424.6 4.5 scatter_fusion
  435.2 4.5 scatter_fusion
  445.7 4.6 scatter_fusion
  456.4 4.5 scatter_fusion
  466.9 4.5 scatter_fusion
  477.5 4.5 scatter_fusion
  488.1 4.6 scatter_fusion
  498.7 4.5 scatter_fusion
  509.2 4.5 scatter_fusion
  519.8 4.4 scatter_fusion
  530.2 4.4 scatter_fusion
  539.0 8.6 %all-to-all-start.1 = ((bf16[16,4,128,256]{3,2,1,0:T(8,128)(2,1)}), bf16[16,4,128,256]{3,2,1,0:T(8,128)(2,1)}, u32[]{:S(2)}, u32[]{:S(2)}) async-start(bf16[16,4,128,256]{3,2,1,0:T(8,128)(2,1)} %get-tuple-element.70), calls=%async_computation.1 | async-start | bytes 8388608 | tf_op jit(solution)/shard_map/all_to_all | solution.py:124
  547.6 6.3 fusion.17
  553.9 87.2 %all-to-all-done.1 = bf16[16,4,128,256]{3,2,1,0:T(8,128)(2,1)} async-done(((bf16[16,4,128,256]{3,2,1,0:T(8,128)(2,1)}), bf16[16,4,128,256]{3,2,1,0:T(8,128)(2,1)}, u32[]{:S(2)}, u32[]{:S(2)}) %all-to-all-start.1) | async-done | bytes 4194336 | tf_op jit(solution)/shard_map/all_to_all | solution.py:124
  641.1 4.5 fusion.23
  (287 shorter events, 179.4 us)
Async XLA Ops:
  7.2 191.7 %copy-start = (bf16[256,1,512]{2,0,1:T(8,128)(2,1)S(1)}, bf16[256,1,512]{2,0,1:T(8,128)(2,1)}, u32[]{:S(2)}) copy-start(bf16[256,1,512]{2,0,1:T(8,128)(2,1)} %param.18) | copy-start | bytes 786436
  15.3 10.2 %copy-start.3 = (s32[256,1,4]{0,2,1:T(4,128)S(1)}, s32[256,1,4]{0,2,1:T(4,128)}, u32[]{:S(2)}) copy-start(s32[256,1,4]{0,2,1:T(4,128)} %param.19) | copy-start | bytes 12292
  15.3 11.0 %copy-start.4 = (s32[256]{0:T(256)S(1)}, s32[256]{0:T(256)}, u32[]{:S(2)}) copy-start(s32[256]{0:T(256)} %param.21) | copy-start | bytes 3076
  15.3 103.6 %all-to-all-start = ((bf16[16,4,128,256]{3,2,1,0:T(8,128)(2,1)}), bf16[16,4,128,256]{3,2,1,0:T(8,128)(2,1)}, u32[]{:S(2)}, u32[]{:S(2)}) async-start(bf16[16,4,128,256]{3,2,1,0:T(8,128)(2,1)} %bitcast.132), calls=%async_computation | async-start | bytes 8388608 | tf_op jit(solution)/shard_map/all_to_all | solution.py:71
  25.4 260.5 %reduce-scatter.4.cloned.1.call-start = ((), (), s32[]{:S(2)}) async-start(), calls=%async_computation.4 | async-start | bytes 8912896
  196.9 0.7 copy-start.1
  197.0 170.7 %all-gather.2.cloned.1.call-start = ((), (), s32[]{:S(2)}) async-start(), calls=%async_computation.3 | async-start | bytes 8912896 | tf_op jit(solution)/shard_map/all_gather | solution.py:108
  539.0 8.6 %copy-start.2 = (bf16[4096,256]{1,0:T(8,128)(2,1)S(1)}, bf16[4096,256]{1,0:T(8,128)(2,1)}, u32[]{:S(2)}) copy-start(bf16[4096,256]{1,0:T(8,128)(2,1)} %param.17) | copy-start | bytes 6291460
  539.0 102.1 %all-to-all-start.1 = ((bf16[16,4,128,256]{3,2,1,0:T(8,128)(2,1)}), bf16[16,4,128,256]{3,2,1,0:T(8,128)(2,1)}, u32[]{:S(2)}, u32[]{:S(2)}) async-start(bf16[16,4,128,256]{3,2,1,0:T(8,128)(2,1)} %get-tuple-element.70), calls=%async_computation.1 | async-start | bytes 8388608 | tf_op jit(solution)/shard_map/all_to_all | solution.py:124
Sparse Core Ops, SparseCore 0:
  197.1 88.7 reduce-scatter.3
  291.1 76.5 all-gather.1
where the time goes:
time: 657 us; the launch traced here: 654 us
  waiting for transfers between devices  342 us (52%)
  local copies, waits for them, and re-layouts  105 us (16%)
  matrix products  87.3 us (13%)
  other arithmetic  85.8 us (13%)
  starting transfers between devices  18.8 us (3%)
  between operations  14.2 us (2%)
    all_to_all x1, waiting for transfers between devices, shards(): lax.all_to_all(outgoing, 'vocab', split_axis=0, concat_axis=0, tiled=True)  91.4 us
    all_to_all x1, waiting for transfers between devices, shards(): lax.all_to_all(returned, 'vocab', split_axis=0, concat_axis=0, tiled=True)  87.2 us
    unnamed x3, waiting for transfers between devices  86.8 us
    all_gather x1, waiting for transfers between devices, shards(): slope_all = lax.all_gather(slope_mine, 'dp', axis=0, tiled=True)  76.7 us
    scatter-add x16, other arithmetic, backward_step(): grad_sum.at[block_ids.reshape(-1)]  71.8 us
    gather x16, local copies, waits for them, and re-layouts, partial_for(): w_sel = w_blocks[block_ids].reshape(OWN_SLOTS, col_width, dslice)  35.3 us
    gather x16, local copies, waits for them, and re-layouts, backward_step(): w_sel = w_blocks[block_ids].reshape(OWN_SLOTS, col_width, dslice)  35.3 us
    dot_general x16, matrix products, backward_step(): jnp.einsum('stc,scd->std', slope, w_sel, preferred_element_type=jnp.float32)  33.1 us
  transfers between devices with their start and end apart: 4, of which 4 were waited for; matrix products, arithmetic and copies ran while one was open for 2% of the time, Pallas kernels for 0%

commit v1 on v0

--- a/solution.py
+++ b/solution.py
@@ -105,7 +105,9 @@
         lax.dynamic_slice_in_dim(col_ok, my_start, my_share, 0),
         lax.dynamic_slice_in_dim(divisor, my_start, my_share, 0),
     )
-    slope_all = lax.all_gather(slope_mine, "dp", axis=0, tiled=True)
+    slope_all = jnp.concatenate(
+        lax.all_to_all(jnp.stack([slope_mine] * lax.axis_size("dp")), "dp", 0, 0), axis=0
+    )
 
     def backward_step(grad_sum, inputs_here):
         slot_rows, block_ids, slope = inputs_here

time: 657 us -> 707 us (1.076)
  waiting for transfers between devices: 342 us -> 386 us
  local copies, waits for them, and re-layouts: 105 us -> 91.6 us
  matrix products: 87.3 us -> 99.7 us
  starting transfers between devices: 18.8 us -> 26.4 us
    all_to_all x0 -> x1, waiting for transfers between devices: none -> 121 us  [shards(): lax.all_to_all(jnp.stack([slope_mine] * lax.axis_size('dp')), 'dp', 0, 0)]
    all_gather x1 -> x0, waiting for transfers between devices: 76.7 us -> none  [shards(): slope_all = lax.all_gather(slope_mine, 'dp', axis=0, tiled=True)]
    dynamic_update_slice x32 -> x0, local copies, waits for them, and re-layouts: 17.9 us -> none  [shards(): partial_value = lax.map(partial_for, (arrived, slot_ids))]
    dot_general x16, matrix products: 22.9 us -> 35.8 us  [partial_for(): jnp.einsum('std,scd->stc', slot_rows, w_sel, preferred_element_type=jnp.f...]
    unnamed x3 -> x2, waiting for transfers between devices: 86.8 us -> 86.6 us
  transfers between devices with their start and end apart: 4 -> 4, of which waited for: 4 -> 4; matrix products, arithmetic and copies ran while one was open for 2% -> 1% of each run, Pallas kernels for 0% -> 0%
where the time goes in v1:
time: 707 us; the launch traced here: 704 us
  waiting for transfers between devices  386 us (55%)
  matrix products  99.7 us (14%)
  local copies, waits for them, and re-layouts  91.6 us (13%)
  other arithmetic  85.5 us (12%)
  starting transfers between devices  26.4 us (4%)
  between operations  14.3 us (2%)
    all_to_all x1, waiting for transfers between devices, shards(): lax.all_to_all(jnp.stack([slope_mine] * lax.axis_size('dp')), 'dp', 0, 0)  121 us
    all_to_all x1, waiting for transfers between devices, shards(): lax.all_to_all(outgoing, 'vocab', split_axis=0, concat_axis=0, tiled=True)  91.4 us
    all_to_all x1, waiting for transfers between devices, shards(): lax.all_to_all(returned, 'vocab', split_axis=0, concat_axis=0, tiled=True)  87.2 us
    unnamed x2, waiting for transfers between devices  86.6 us
    scatter-add x16, other arithmetic, backward_step(): grad_sum.at[block_ids.reshape(-1)]  72.3 us
    dot_general x16, matrix products, partial_for(): jnp.einsum('std,scd->stc', slot_rows, w_sel, preferred_element_type=jnp.f...  35.8 us
    gather x16, local copies, waits for them, and re-layouts, partial_for(): w_sel = w_blocks[block_ids].reshape(OWN_SLOTS, col_width, dslice)  35.3 us
    gather x16, local copies, waits for them, and re-layouts, backward_step(): w_sel = w_blocks[block_ids].reshape(OWN_SLOTS, col_width, dslice)  35.3 us
  transfers between devices with their start and end apart: 4, of which 4 were waited for; matrix products, arithmetic and copies ran while one was open for 1% of the time, Pallas kernels for 0%

profile of v1, /device:TPU:1, one launch (start us, length us, event | category | flops | bytes accessed | tf_op | source)
XLA Modules:
  0.0 703.7 jit_solution(12581342079753632725)
XLA Ops:
  12.3 3.1 copy.58
  15.4 10.1 %all-to-all-start = ((bf16[16,4,128,256]{3,2,1,0:T(8,128)(2,1)}), bf16[16,4,128,256]{3,2,1,0:T(8,128)(2,1)}, u32[]{:S(2)}, u32[]{:S(2)}) async-start(bf16[16,4,128,256]{3,2,1,0:T(8,128)(2,1)} %bitcast.135), calls=%async_computation | async-start | bytes 8388608 | tf_op jit(solution)/shard_map/all_to_all | solution.py:71
  27.6 91.4 %all-to-all-done = bf16[16,4,128,256]{3,2,1,0:T(8,128)(2,1)} async-done(((bf16[16,4,128,256]{3,2,1,0:T(8,128)(2,1)}), bf16[16,4,128,256]{3,2,1,0:T(8,128)(2,1)}, u32[]{:S(2)}, u32[]{:S(2)}) %all-to-all-start) | async-done | bytes 4194336 | tf_op jit(solution)/shard_map/all_to_all | solution.py:71
  119.0 72.8 %while.22 = (s32[]{:T(128)}, bf16[16,4,128,512]{3,2,1,0:T(8,128)(2,1)}, bf16[16,4,128,256]{3,2,1,0:T(8,128)(2,1)}, s32[16,4,4]{2,1,0:T(4,128)S(1)}, bf16[32,128,256]{2,1,0:T(8,128)(2,1)}, /*index=5*/s32[]{:T(128)}) while((s32[]{:T(128)}, bf16[16,4,128,512]{3,2,1,0:T(8,128)(2,1)}, bf16[16,4,128,256]{3,2,1,0:T(8,128)(2,1)}, ...), condition=%wide.region_3.4_spmd, body=%wide.region_2.3_spmd.sunk | while | flops 134480944 | bytes 3937737 | solution.py:94
  162.2 2.3 fusion.59
  194.0 86.6 %reduce-scatter.4.cloned.1.call-done = bf16[1,4,128,512]{3,2,1,0:T(8,128)(2,1)} async-done(((bf16[16,4,128,512]{3,2,1,0:T(8,128)(2,1)}), bf16[1,4,128,512]{3,2,1,0:T(8,128)(2,1)}) %reduce-scatter.4.cloned.1.call-update) | async-done | bytes 524304
  280.5 3.1 fusion.28
  283.9 5.2 stack.2
  289.1 4.7 all-to-all-start.1
  293.9 120.7 %all-to-all-done.1 = bf16[16,1,4,128,512]{3,4,2,1,0:T(8,128)(2,1)} async-done(((bf16[16,1,4,128,512]{3,4,2,1,0:T(8,128)(2,1)}), bf16[16,1,4,128,512]{3,4,2,1,0:T(8,128)(2,1)}, u32[]{:S(2)}, u32[]{:S(2)}) %all-to-all-start.1) | async-done | bytes 8388640 | tf_op jit(solution)/shard_map/all_to_all | solution.py:109
  414.6 2.5 broadcast_in_dim.23
  417.0 169.0 %while.23 = (s32[]{:T(128)}, f32[32,128,256]{2,1,0:T(8,128)}, bf16[16,4,128,256]{3,2,1,0:T(8,128)(2,1)}, s32[16,4,4]{2,1,0:T(4,128)S(1)}, bf16[16,4,128,512]{2,3...) while((s32[]{:T(128)}, f32[32,128,256]{2,1,0:T(8,128)}, ...), condition=%wide.region_11.12_spmd, body=%wide.region_9.11_spmd.sunk | while | flops 269091936 | bytes 13114201 | solution.py:125
  418.7 4.5 scatter_fusion
  429.2 4.4 scatter_fusion
  439.7 4.7 scatter_fusion
  450.4 4.7 scatter_fusion
  461.2 4.4 scatter_fusion
  471.6 4.4 scatter_fusion
  482.1 4.5 scatter_fusion
  492.7 4.6 scatter_fusion
  503.3 4.5 scatter_fusion
  513.9 4.5 scatter_fusion
  524.4 4.6 scatter_fusion
  535.0 4.6 scatter_fusion
  545.6 4.6 scatter_fusion
  556.3 4.5 scatter_fusion
  566.8 4.4 scatter_fusion
  577.2 4.4 scatter_fusion
  586.0 11.5 %all-to-all-start.2 = ((bf16[16,4,128,256]{3,2,1,0:T(8,128)(2,1)}), bf16[16,4,128,256]{3,2,1,0:T(8,128)(2,1)}, u32[]{:S(2)}, u32[]{:S(2)}) async-start(bf16[16,4,128,256]{3,2,1,0:T(8,128)(2,1)} %get-tuple-element.70), calls=%async_computation.2 | async-start | bytes 8388608 | tf_op jit(solution)/shard_map/all_to_all | solution.py:126
  597.5 6.3 fusion.18
  603.8 87.2 %all-to-all-done.2 = bf16[16,4,128,256]{3,2,1,0:T(8,128)(2,1)} async-done(((bf16[16,4,128,256]{3,2,1,0:T(8,128)(2,1)}), bf16[16,4,128,256]{3,2,1,0:T(8,128)(2,1)}, u32[]{:S(2)}, u32[]{:S(2)}) %all-to-all-start.2) | async-done | bytes 4194336 | tf_op jit(solution)/shard_map/all_to_all | solution.py:126
  691.0 4.5 fusion.24
  (257 shorter events, 177.6 us)
Async XLA Ops:
  7.2 186.5 %copy-start = (bf16[256,1,512]{2,0,1:T(8,128)(2,1)S(1)}, bf16[256,1,512]{2,0,1:T(8,128)(2,1)}, u32[]{:S(2)}) copy-start(bf16[256,1,512]{2,0,1:T(8,128)(2,1)} %param.18) | copy-start | bytes 786436
  15.3 11.0 %copy-start.5 = (s32[256]{0:T(256)S(1)}, s32[256]{0:T(256)}, u32[]{:S(2)}) copy-start(s32[256]{0:T(256)} %param.21) | copy-start | bytes 3076
  15.4 11.7 %copy-start.4 = (s32[256,1,4]{0,2,1:T(4,128)S(1)}, s32[256,1,4]{0,2,1:T(4,128)}, u32[]{:S(2)}) copy-start(s32[256,1,4]{0,2,1:T(4,128)} %param.19) | copy-start | bytes 12292
  15.4 103.6 %all-to-all-start = ((bf16[16,4,128,256]{3,2,1,0:T(8,128)(2,1)}), bf16[16,4,128,256]{3,2,1,0:T(8,128)(2,1)}, u32[]{:S(2)}, u32[]{:S(2)}) async-start(bf16[16,4,128,256]{3,2,1,0:T(8,128)(2,1)} %bitcast.135), calls=%async_computation | async-start | bytes 8388608 | tf_op jit(solution)/shard_map/all_to_all | solution.py:71
  25.5 255.1 %reduce-scatter.4.cloned.1.call-start = ((), (), s32[]{:S(2)}) async-start(), calls=%async_computation.4 | async-start | bytes 8912896
  191.8 0.7 copy-start.2
  289.1 125.4 %all-to-all-start.1 = ((bf16[16,1,4,128,512]{3,4,2,1,0:T(8,128)(2,1)}), bf16[16,1,4,128,512]{3,4,2,1,0:T(8,128)(2,1)}, u32[]{:S(2)}, u32[]{:S(2)}) async-start(bf16[16,1,4,128,512]{3,4,2,1,0:T(8,128)(2,1)} %stack.2), calls=%async_computation.1 | async-start | bytes 16777216 | tf_op jit(solution)/shard_map/all_to_all | solution.py:109
  586.0 11.5 %copy-start.3 = (bf16[4096,256]{1,0:T(8,128)(2,1)S(1)}, bf16[4096,256]{1,0:T(8,128)(2,1)}, u32[]{:S(2)}) copy-start(bf16[4096,256]{1,0:T(8,128)(2,1)} %param.17) | copy-start | bytes 6291460
  586.0 105.0 %all-to-all-start.2 = ((bf16[16,4,128,256]{3,2,1,0:T(8,128)(2,1)}), bf16[16,4,128,256]{3,2,1,0:T(8,128)(2,1)}, u32[]{:S(2)}, u32[]{:S(2)}) async-start(bf16[16,4,128,256]{3,2,1,0:T(8,128)(2,1)} %get-tuple-element.70), calls=%async_computation.2 | async-start | bytes 8388608 | tf_op jit(solution)/shard_map/all_to_all | solution.py:126
  597.5 99.4 %copy-start.1 = (bf16[256,1,512]{2,0,1:T(8,128)(2,1)S(1)}, bf16[256,1,512]{2,0,1:T(8,128)(2,1)}, u32[]{:S(2)}) copy-start(bf16[256,1,512]{2,0,1:T(8,128)(2,1)} %param.18) | copy-start | bytes 786436
Sparse Core Ops, SparseCore 0:
  191.9 88.5 reduce-scatter.3
